TPU v7x, 128 devices: a whole 4x4x4 slice. The times are simulated.
128 devices in a mesh: mem: 16 (over z, x), sub: 8 (over y, core).
Axes of the slice: x: 4, y: 4, z: 4, core: 2. Of those that a mesh axis runs over, the one named last changes fastest.
Arguments:
- ensemble: float32 [64, 3, 256, 2048], P('mem', None, 'sub'), may hold values from -6 to 6
- sea_depth: float32 [256, 2048], P('sub'), may hold values from 0.5 to 2
- cutoff: int32 [256, 2048], P('sub', 'mem'), may hold values from 16 to 64
- obs_index: int32 [4, 256], replicated, may hold values from 0 to 524287
- obs_value: float32 [4, 256], replicated, may hold values from -6 to 6
- obs_var: float32 [4, 256], replicated, may hold values from 0.5 to 2
Outputs:
- analysis: float32 [64, 3, 256, 2048], P(None, None, 'sub', 'mem')
All inputs are finite; a program needn't handle non-finite values.
Results may differ from a plain program's by a relative error of at most 0.0001.
Values sent between devices are 32-bit elements; how exact they have to be, the bound alone decides.
A program may use at most 192 MiB of HBM per device.

v0:
```python
import jax
import jax.numpy as jnp
from jax import lax
from jax.sharding import PartitionSpec as P

STEPS = 4
BATCHES = 4
step_size = 0.3
coriolis = 0.2
highest = lax.Precision.HIGHEST


def padded(shard, sides, width):
    for axis, dim in sides:
        peers, length = (lax.axis_size(axis), shard.shape[dim])
        up = [(i, (i + 1) % peers) for i in range(peers)]
        down = [(j, i) for i, j in up]
        last = lax.slice_in_dim(shard, length - width, length, axis=dim)
        leading = lax.slice_in_dim(shard, 0, width, axis=dim)
        before = lax.ppermute(last, axis, up)
        after = lax.ppermute(leading, axis, down)
        shard = jnp.concatenate([before, shard, after], axis=dim)
    return shard


def across_cols(field):
    return (jnp.roll(field, -1, 2) - jnp.roll(field, 1, 2)) * 0.5


def momentum(height, east_wind, north_wind):
    height_ext = padded(height, (("sub", 1),), 1)
    height_dx = (height_ext[:, 2:] - height_ext[:, :-2]) * 0.5
    east_new = east_wind + step_size * (coriolis * north_wind - height_dx)
    north_new = north_wind + step_size * (-coriolis * east_wind - across_cols(height))
    return (east_new, north_new)


def continuity(height, east_wind, north_wind, sea_depth):
    flux_ext = padded(sea_depth * east_wind, (("sub", 1),), 1)
    divergence = (flux_ext[:, 2:] - flux_ext[:, :-2]) * 0.5 + across_cols(sea_depth * north_wind)
    return height - step_size * divergence


def localize(obs_x, obs_y, cell_x, cell_y, radius_sq, size_x, size_y):
    gap_x = jnp.abs(cell_x[None, :] - obs_x[:, None])
    gap_x = jnp.minimum(gap_x, size_x - gap_x)
    gap_y = jnp.abs(cell_y[None, :] - obs_y[:, None])
    gap_y = jnp.minimum(gap_y, size_y - gap_y)
    dist_sq = (gap_x * gap_x + gap_y * gap_y).astype(jnp.float32)
    dist_ratio = dist_sq / radius_sq[None, :]
    return jnp.square(jnp.maximum(1.0 - dist_ratio, 0.0))


def analysis_weights(prior_obs, values, variance):
    member_count = prior_obs.shape[1]
    obs_mean = jnp.mean(prior_obs, 1)
    obs_anom = prior_obs - obs_mean[:, None]
    innov_cov = jnp.dot(obs_anom, obs_anom.T, precision=highest) / (member_count - 1) + jnp.diag(
        variance
    )
    factor = jnp.linalg.cholesky(innov_cov)
    right_side = jnp.concatenate([(values - obs_mean)[:, None], obs_anom], 1)
    solved = jax.scipy.linalg.cho_solve((factor, True), right_side)
    return (obs_anom, solved[:, :1] - 0.5 * solved[:, 1:])


def update_state(members, obs_anom, weights_mix, loc_weight, cell_count):
    member_count = members.shape[0]
    obs_count = obs_anom.shape[0]
    state_anom = members - jnp.mean(members, 0)
    cross_cov = jnp.dot(obs_anom, state_anom, precision=highest) / (member_count - 1)
    loc_gain = (cross_cov.reshape(obs_count, 3, cell_count) * loc_weight[:, None, :]).reshape(
        obs_count, 3 * cell_count
    )
    return members + jnp.dot(weights_mix.T, loc_gain, precision=highest)


def local(ensemble, sea_depth, cutoff, obs_index, obs_value, obs_var):
    height = ensemble[:, 0]
    east_wind = ensemble[:, 1]
    north_wind = ensemble[:, 2]
    for step_id in range(STEPS - 1):
        east_wind, north_wind = momentum(height, east_wind, north_wind)
        height = continuity(height, east_wind, north_wind, sea_depth)
    east_wind, north_wind = momentum(height, east_wind, north_wind)
    height = continuity(height, east_wind, north_wind, sea_depth)
    point_state = lax.all_to_all(
        jnp.stack([height, east_wind, north_wind], 1),
        "mem",
        split_axis=3,
        concat_axis=0,
        tiled=True,
    )
    member_count = point_state.shape[0]
    row_count, col_block = cutoff.shape
    x_start = lax.axis_index("sub") * row_count
    y_start = lax.axis_index("mem") * col_block
    size_x = row_count * lax.axis_size("sub")
    size_y = col_block * lax.axis_size("mem")
    cell_count = row_count * col_block
    cell_ids = jnp.arange(cell_count, dtype=jnp.int32)
    cell_x = x_start + cell_ids // col_block
    cell_y = y_start + cell_ids % col_block
    radius_sq = jnp.square(cutoff.reshape(cell_count).astype(jnp.float32))
    members = point_state.reshape(member_count, 3 * cell_count)
    for batch_id in range(BATCHES):
        obs_cell = obs_index[batch_id]
        obs_x = obs_cell // size_y
        obs_y = obs_cell % size_y
        select_obs_x = obs_cell // size_y
        select_obs_y = obs_cell % size_y
        inside = (
            (select_obs_x >= x_start)
            & (select_obs_x < x_start + row_count)
            & (select_obs_y >= y_start)
            & (select_obs_y < y_start + col_block)
        )
        local_id = (select_obs_x - x_start) * col_block + (select_obs_y - y_start)
        local_part = lax.dot_general(
            ((local_id[:, None] == cell_ids[None, :]) & inside[:, None]).astype(jnp.float32),
            members[:, :cell_count],
            (((1,), (1,)), ((), ())),
            precision=highest,
        )
        prior_obs = lax.psum(local_part, ("mem", "sub"))
        obs_anom, weights_mix = analysis_weights(prior_obs, obs_value[batch_id], obs_var[batch_id])
        loc_weight = localize(obs_x, obs_y, cell_x, cell_y, radius_sq, size_x, size_y)
        members = update_state(members, obs_anom, weights_mix, loc_weight, cell_count)
    return members.reshape(member_count, 3, row_count, col_block)


def solution(mesh):
    return jax.shard_map(
        local,
        mesh=mesh,
        in_specs=(P("mem", None, "sub", None), P("sub", None), P("sub", "mem"), P(), P(), P()),
        out_specs=P(None, None, "sub", "mem"),
        check_vma=False,
    )
```

profile of v0, /device:TPU:1, one launch (start us, length us, event | category | flops | bytes accessed | tf_op | source)
XLA Modules:
  0.0 1229.5 jit_solution(545508524932749431)
XLA Ops:
  18.8 5.2 broadcast_multiply_fusion.7
  74.6 8.9 copy.119
  83.5 15.4 %reshape.856 = f32[16,1,49152]{2,1,0:T(1,128)} reshape(f32[2048,3,4,32]{3,2,1,0:T(4,128)} %bitcast.231) | data formatting | bytes 6291456
  99.0 7.6 all-to-all-start
  106.8 14.0 %fusion.34 = (f32[256,4096]{0,1:T(8,128)}, f32[256,4096]{0,1:T(8,128)}, f32[256,4096]{0,1:T(8,128)}, f32[256,4096]{0,1:T(8,128)S(1)}) fusion(s32[256]{0:T(256)S(1)} %copy-done.18, s32[256]{0:T(256)S(1)} %copy-done.17, f32[4096]{0:T(1024)S(1)} %multiply_bitcast_fusion, s32[4096]{0:T(1024)S(1)} %copy-done.16, s32[4096]{0:T(1024)S(1)} %copy-done.15, ...), kind=kLoop, calls=%fused_computation.58 | loop fusion | flops 67108864 | bytes 16834560 | tf_op jit(solution)/shard_map/square | solution.py:51
  120.7 5.6 mul.346
  126.4 12.6 %copy.123 = f32[256,12288]{1,0:T(8,128)} copy(f32[256,12288]{0,1:T(8,128)} %bitcast.227) | data formatting | bytes 25165824 | tf_op jit(solution)/shard_map/mul | solution.py:72
  139.0 7.8 mul.353
  146.8 12.6 %copy.126 = f32[256,12288]{1,0:T(8,128)} copy(f32[256,12288]{0,1:T(8,128)} %bitcast.228) | data formatting | bytes 25165824 | tf_op jit(solution)/shard_map/mul | solution.py:72
  159.4 7.8 mul.360
  167.2 12.6 %copy.129 = f32[256,12288]{1,0:T(8,128)} copy(f32[256,12288]{0,1:T(8,128)} %bitcast.229) | data formatting | bytes 25165824 | tf_op jit(solution)/shard_map/mul | solution.py:72
  179.8 7.8 mul.367
  187.5 12.8 %copy.132 = f32[256,12288]{1,0:T(8,128)} copy(f32[256,12288]{0,1:T(8,128)} %bitcast.230) | data formatting | bytes 25165824 | tf_op jit(solution)/shard_map/mul | solution.py:72
  203.2 10.8 reduce.9
  214.1 15.0 %reshape.857 = f32[2048,3,4,32]{3,2,1,0:T(4,128)} reshape(f32[16,49152]{1,0:T(8,128)} %reduce.9) | data formatting | bytes 6291456
  229.1 9.9 copy.120
  247.5 141.1 %all-reduce.6.cloned.1.call-done = f32[256,64]{0,1:T(8,128)} async-done(((f32[256,64]{0,1:T(8,128)}), f32[256,64]{0,1:T(8,128)}) %all-reduce.6.cloned.1.call-update) | async-done | bytes 65552 | tf_op jit(solution)/shard_map/psum | solution.py:125
  393.3 11.7 cholesky.214
  406.2 10.6 custom-call.19
  419.7 12.5 %cholesky.231 = f32[128,128]{1,0:T(8,128)S(1)} custom-call(f32[128,128]{1,0:T(8,128)} %convolution_subtract_fusion.3), custom_call_target="Cholesky" | custom-call | tf_op jit(solution)/shard_map/jit(cholesky)/cholesky | solution.py:61
  437.3 5.4 while.8
  442.7 21.1 %custom-call.20 = f32[2,128,128]{1,2,0:T(8,128)} custom-call(f32[2,128,128]{2,1,0:T(8,128)} %get-tuple-element.33), custom_call_target="InvertDiagBlocksLowerTriangular" | custom-call | tf_op jit(solution)/shard_map/jit(_cho_solve)/triangular_solve | solution.py:63
  469.3 13.6 %fusion.3 = f32[256,12288]{1,0:T(8,128)S(1)} fusion(f32[256,12288]{1,0:T(8,128)} %copy.123, f32[256,64]{0,1:T(8,128)S(1)} %broadcast_subtract_fusion.3, f32[64,12288]{1,0:T(8,128)S(1)} %reshape.826, f32[12288]{0:T(1024)} %bitcast.240), kind=kOutput, calls=%fused_computation.15 | convolution fusion | flops 2422996992 | bytes 28426240 | tf_op jit(solution)/shard_map/dot_general | solution.py:71
  483.0 9.6 fusion.258
  496.6 135.9 %all-reduce.8.cloned.1.call-done = f32[256,64]{0,1:T(8,128)} async-done(((f32[256,64]{0,1:T(8,128)}), f32[256,64]{0,1:T(8,128)}) %all-reduce.8.cloned.1.call-update) | async-done | bytes 65552 | tf_op jit(solution)/shard_map/psum | solution.py:125
  637.2 11.7 cholesky.248
  649.6 10.6 custom-call.21
  663.0 12.5 %cholesky.265 = f32[128,128]{1,0:T(8,128)S(1)} custom-call(f32[128,128]{1,0:T(8,128)} %convolution_subtract_fusion.2), custom_call_target="Cholesky" | custom-call | tf_op jit(solution)/shard_map/jit(cholesky)/cholesky | solution.py:61
  679.7 6.5 while.9
  686.1 21.1 %custom-call.22 = f32[2,128,128]{1,2,0:T(8,128)} custom-call(f32[2,128,128]{2,1,0:T(8,128)} %get-tuple-element.34), custom_call_target="InvertDiagBlocksLowerTriangular" | custom-call | tf_op jit(solution)/shard_map/jit(_cho_solve)/triangular_solve | solution.py:63
  712.7 13.6 %fusion.2 = f32[256,12288]{1,0:T(8,128)S(1)} fusion(f32[256,12288]{1,0:T(8,128)} %copy.126, f32[256,64]{0,1:T(8,128)S(1)} %broadcast_subtract_fusion.2, f32[64,12288]{1,0:T(8,128)S(1)} %get-tuple-element.195, f32[12288]{0:T(1024)} %broadcast_multiply_fusion.10), kind=kOutput, calls=%fused_computation.13 | convolution fusion | flops 2422996992 | bytes 28426240 | tf_op jit(solution)/shard_map/dot_general | solution.py:71
  726.4 8.0 fusion.259
  740.1 135.9 %all-reduce.10.cloned.1.call-done = f32[256,64]{0,1:T(8,128)} async-done(((f32[256,64]{0,1:T(8,128)}), f32[256,64]{0,1:T(8,128)}) %all-reduce.10.cloned.1.call-update) | async-done | bytes 65552 | tf_op jit(solution)/shard_map/psum | solution.py:125
  880.7 11.7 cholesky.282
  893.1 10.6 custom-call.23
  906.5 12.5 %cholesky.299 = f32[128,128]{1,0:T(8,128)S(1)} custom-call(f32[128,128]{1,0:T(8,128)} %convolution_subtract_fusion.1), custom_call_target="Cholesky" | custom-call | tf_op jit(solution)/shard_map/jit(cholesky)/cholesky | solution.py:61
  923.4 6.6 while.10
  929.9 21.1 %custom-call.24 = f32[2,128,128]{1,2,0:T(8,128)} custom-call(f32[2,128,128]{2,1,0:T(8,128)} %get-tuple-element.35), custom_call_target="InvertDiagBlocksLowerTriangular" | custom-call | tf_op jit(solution)/shard_map/jit(_cho_solve)/triangular_solve | solution.py:63
  955.9 13.6 %fusion.1 = f32[256,12288]{1,0:T(8,128)S(1)} fusion(f32[256,12288]{1,0:T(8,128)} %copy.129, f32[256,64]{0,1:T(8,128)S(1)} %broadcast_subtract_fusion.1, f32[64,12288]{1,0:T(8,128)S(1)} %copy-done.1, f32[12288]{0:T(1024)} %broadcast_multiply_fusion.9), kind=kOutput, calls=%fused_computation.11 | convolution fusion | flops 2422996992 | bytes 28426240 | tf_op jit(solution)/shard_map/dot_general | solution.py:71
  969.5 8.0 fusion.260
  982.9 136.2 %all-reduce.12.cloned.1.call-done = f32[256,64]{0,1:T(8,128)} async-done(((f32[256,64]{0,1:T(8,128)}), f32[256,64]{0,1:T(8,128)}) %all-reduce.12.cloned.1.call-update) | async-done | bytes 65552 | tf_op jit(solution)/shard_map/psum | solution.py:125
  1123.8 11.8 cholesky.316
  1136.3 10.6 custom-call.25
  1149.8 12.5 %cholesky.333 = f32[128,128]{1,0:T(8,128)S(1)} custom-call(f32[128,128]{1,0:T(8,128)} %convolution_subtract_fusion), custom_call_target="Cholesky" | custom-call | tf_op jit(solution)/shard_map/jit(cholesky)/cholesky | solution.py:61
  1166.5 6.6 while.11
  1173.2 21.1 %custom-call.26 = f32[2,128,128]{1,2,0:T(8,128)} custom-call(f32[2,128,128]{2,1,0:T(8,128)} %get-tuple-element.36), custom_call_target="InvertDiagBlocksLowerTriangular" | custom-call | tf_op jit(solution)/shard_map/jit(_cho_solve)/triangular_solve | solution.py:63
  1199.1 13.4 %fusion = f32[256,12288]{1,0:T(8,128)S(1)} fusion(f32[256,12288]{1,0:T(8,128)} %copy.132, f32[256,64]{0,1:T(8,128)S(1)} %broadcast_subtract_fusion, f32[64,12288]{1,0:T(8,128)S(1)} %copy-done.5, f32[12288]{0:T(1024)} %broadcast_multiply_fusion.8), kind=kOutput, calls=%fused_computation.9 | convolution fusion | flops 2422996992 | bytes 28426240 | tf_op jit(solution)/shard_map/dot_general | solution.py:71
  1212.5 7.9 fusion.60
  (291 shorter events, 182.1 us)
Async XLA Ops:
  9.6 6.1 copy-start.26
  9.6 9.2 copy-start.6
  10.9 7.9 collective-permute-start
  12.3 6.5 collective-permute-start.1
  24.7 3.4 collective-permute-start.2
  26.0 3.7 collective-permute-start.3
  31.8 4.7 collective-permute-start.4
  35.6 1.2 collective-permute-start.5
  40.0 4.2 collective-permute-start.6
  43.4 1.2 collective-permute-start.7
  46.3 4.2 collective-permute-start.8
  49.7 1.2 collective-permute-start.9
  54.2 4.2 collective-permute-start.10
  57.5 1.2 collective-permute-start.11
  60.5 4.2 collective-permute-start.12
  63.8 1.2 collective-permute-start.13
  68.2 4.2 collective-permute-start.14
  71.6 1.2 collective-permute-start.15
  98.9 7.7 copy-start.15
  98.9 7.7 copy-start.16
  98.9 7.8 copy-start.17
  98.9 7.8 copy-start.18
  98.9 7.8 copy-start.19
  98.9 7.8 copy-start.20
  98.9 7.8 copy-start.21
  99.0 7.8 copy-start.22
  99.0 7.8 copy-start.23
  99.0 7.8 copy-start.24
  99.0 103.7 %all-to-all-start = ((f32[16,1,49152]{2,1,0:T(1,128)}), f32[16,1,49152]{2,1,0:T(1,128)S(1)}, u32[]{:S(2)}, u32[]{:S(2)}) async-start(f32[16,1,49152]{2,1,0:T(1,128)} %reshape.856), calls=%async_computation | async-start | bytes 6291456 | tf_op jit(solution)/shard_map/all_to_all | solution.py:87
  106.6 282.0 %all-reduce.6.cloned.1.call-start = ((), (), s32[]{:S(2)}) async-start(), calls=%async_computation.1 | async-start | bytes 131072 | tf_op jit(solution)/shard_map/psum | solution.py:125
  187.5 15.1 %copy-start.27 = (f32[4,256]{1,0:T(4,128)S(1)}, f32[4,256]{1,0:T(4,128)}, u32[]{:S(2)}) copy-start(f32[4,256]{1,0:T(4,128)} %param.14) | copy-start | bytes 12292
  239.0 4.5 copy-start.34
  243.5 225.8 %copy-start.2 = (f32[64,12288]{1,0:T(8,128)}, f32[64,12288]{1,0:T(8,128)S(1)}, u32[]{:S(2)}) copy-start(f32[64,12288]{1,0:T(8,128)S(1)} %reshape.826) | copy-start | bytes 9437188
  246.7 385.8 %all-reduce.8.cloned.1.call-start = ((), (), s32[]{:S(2)}) async-start(), calls=%async_computation.2 | async-start | bytes 131072 | tf_op jit(solution)/shard_map/psum | solution.py:125
  432.3 2.6 copy-start.7
  442.7 40.3 %copy-start.35 = (s32[2,2]{1,0:T(2,128)}, s32[2,2]{1,0:T(2,128)S(1)}, u32[]{:S(2)}) copy-start(s32[2,2]{1,0:T(2,128)S(1)} %get-tuple-element.440) | copy-start | bytes 52
  483.0 9.6 copy-start.30
  483.0 9.6 copy-start.33
  495.7 380.3 %all-reduce.10.cloned.1.call-start = ((), (), s32[]{:S(2)}) async-start(), calls=%async_computation.3 | async-start | bytes 131072 | tf_op jit(solution)/shard_map/psum | solution.py:125
  726.4 9.7 copy-start.29
  726.4 9.7 copy-start.32
  734.4 216.7 %copy-start.25 = (f32[4,256]{1,0:T(4,128)S(1)}, f32[4,256]{1,0:T(4,128)}, u32[]{:S(2)}) copy-start(f32[4,256]{1,0:T(4,128)} %param.13) | copy-start | bytes 12292
  739.2 216.7 %copy-start.1 = (f32[64,12288]{1,0:T(8,128)S(1)}, f32[64,12288]{1,0:T(8,128)}, u32[]{:S(2)}) copy-start(f32[64,12288]{1,0:T(8,128)} %copy-done) | copy-start | bytes 9437188
  739.2 379.9 %all-reduce.12.cloned.1.call-start = ((), (), s32[]{:S(2)}) async-start(), calls=%async_computation.4 | async-start | bytes 131072 | tf_op jit(solution)/shard_map/psum | solution.py:125
  919.1 2.6 copy-start.9
  969.5 9.7 copy-start.28
  969.5 9.7 copy-start.31
  982.3 216.8 %copy-start.5 = (f32[64,12288]{1,0:T(8,128)S(1)}, f32[64,12288]{1,0:T(8,128)}, u32[]{:S(2)}) copy-start(f32[64,12288]{1,0:T(8,128)} %copy-done.4) | copy-start | bytes 9437188
  (9 other events, 12.8 us)
Sparse Core Ops, SparseCore 0:
  246.8 141.7 all-reduce.5
  495.8 136.6 all-reduce.7
  739.3 136.6 all-reduce.9
  982.4 136.6 all-reduce.11
where the time goes:
time: 1240 us; the launch traced here: 1230 us
  waiting for transfers between devices  559 us (45%)
  other arithmetic  300 us (24%)
  local copies, waits for them, and re-layouts  185 us (15%)
  matrix products  132 us (11%)
  starting transfers between devices  33.5 us (3%)
  between operations  19.3 us (2%)
    psum x4, waiting for transfers between devices, local(): prior_obs = lax.psum(local_part, ('mem', 'sub'))  549 us
    another operation x27, other arithmetic, analysis_weights(): factor = jnp.linalg.cholesky(innov_cov)  148 us
    another operation x9, other arithmetic, analysis_weights(): solved = jax.scipy.linalg.cho_solve((factor, True), right_side)  88.9 us
    mul x8, local copies, waits for them, and re-layouts, update_state(): cross_cov.reshape(obs_count, 3, cell_count) * loc_weight[:, None, :]  79.6 us
    dot_general x4, matrix products, update_state(): jnp.dot(obs_anom, state_anom, precision=highest) / (member_count - 1)  54.3 us
    unnamed x76, local copies, waits for them, and re-layouts  41 us
    dot_general x4, matrix products, update_state(): return members + jnp.dot(weights_mix.T, loc_gain, precision=highest)  33.4 us
    another operation x29, local copies, waits for them, and re-layouts, analysis_weights(): solved = jax.scipy.linalg.cho_solve((factor, True), right_side)  27.8 us
  transfers between devices with their start and end apart: 21, of which 18 were waited for; matrix products, arithmetic and copies ran while one was open for 8% of the time, Pallas kernels for 0%

commit v1 on v0

--- a/solution.py
+++ b/solution.py
@@ -122,7 +122,8 @@
             (((1,), (1,)), ((), ())),
             precision=highest,
         )
-        prior_obs = lax.psum(local_part, ("mem", "sub"))
+        parts = lax.all_gather(local_part, ("mem", "sub"))
+        prior_obs = jnp.sum(parts, axis=0)
         obs_anom, weights_mix = analysis_weights(prior_obs, obs_value[batch_id], obs_var[batch_id])
         loc_weight = localize(obs_x, obs_y, cell_x, cell_y, radius_sq, size_x, size_y)
         members = update_state(members, obs_anom, weights_mix, loc_weight, cell_count)

time: 1240 us -> 961 us (0.78)
  waiting for transfers between devices: 559 us -> 241 us
  local copies, waits for them, and re-layouts: 185 us -> 205 us
  other arithmetic: 300 us -> 316 us
    psum x4 -> x0, waiting for transfers between devices: 549 us -> none  [local(): prior_obs = lax.psum(local_part, ('mem', 'sub'))]
    all_gather x0 -> x4, waiting for transfers between devices: none -> 195 us  [local(): parts = lax.all_gather(local_part, ('mem', 'sub'))]
    all_to_all x1, waiting for transfers between devices: 0.01 us -> 37.6 us  [local(): lax.all_to_all(jnp.stack([height, east_wind, north_wind], 1), 'mem', spli...]
    unnamed x76 -> x66, local copies, waits for them, and re-layouts: 41 us -> 61.3 us
    reduce_sum x4 -> x8, other arithmetic: 3.45 us -> 16.1 us  [analysis_weights(): obs_mean = jnp.mean(prior_obs, 1)]
  transfers between devices with their start and end apart: 21 -> 21, of which waited for: 18 -> 21; matrix products, arithmetic and copies ran while one was open for 8% -> 11% of each run, Pallas kernels for 0% -> 0%
where the time goes in v1:
time: 961 us; the launch traced here: 949 us
  other arithmetic  316 us (33%)
  waiting for transfers between devices  241 us (25%)
  local copies, waits for them, and re-layouts  205 us (21%)
  matrix products  133 us (14%)
  starting transfers between devices  34.9 us (4%)
  between operations  19.2 us (2%)
    all_gather x4, waiting for transfers between devices, local(): parts = lax.all_gather(local_part, ('mem', 'sub'))  195 us
    another operation x27, other arithmetic, analysis_weights(): factor = jnp.linalg.cholesky(innov_cov)  150 us
    another operation x9, other arithmetic, analysis_weights(): solved = jax.scipy.linalg.cho_solve((factor, True), right_side)  88.9 us
    mul x8, local copies, waits for them, and re-layouts, update_state(): cross_cov.reshape(obs_count, 3, cell_count) * loc_weight[:, None, :]  79.2 us
    unnamed x66, local copies, waits for them, and re-layouts  61.3 us
    dot_general x4, matrix products, update_state(): jnp.dot(obs_anom, state_anom, precision=highest) / (member_count - 1)  53.1 us
    all_to_all x1, waiting for transfers between devices, local(): lax.all_to_all(jnp.stack([height, east_wind, north_wind], 1), 'mem', spli...  37.6 us
    dot_general x4, matrix products, update_state(): return members + jnp.dot(weights_mix.T, loc_gain, precision=highest)  35.1 us
  transfers between devices with their start and end apart: 21, of which 21 were waited for; matrix products, arithmetic and copies ran while one was open for 11% of the time, Pallas kernels for 0%

profile of v1, /device:TPU:1, one launch (start us, length us, event | category | flops | bytes accessed | tf_op | source)
XLA Modules:
  0.0 948.9 jit_solution(3183924278917942165)
XLA Ops:
  68.5 9.0 copy.123
  77.5 15.4 %reshape.864 = f32[16,1,49152]{2,1,0:T(1,128)} reshape(f32[2048,3,4,32]{3,2,1,0:T(4,128)} %bitcast.251) | data formatting | bytes 6291456
  92.9 7.7 all-to-all-start
  100.9 37.6 %all-to-all-done = f32[16,1,49152]{2,1,0:T(1,128)S(1)} async-done(((f32[16,1,49152]{2,1,0:T(1,128)}), f32[16,1,49152]{2,1,0:T(1,128)S(1)}, u32[]{:S(2)}, u32[]{:S(2)}) %all-to-all-start) | async-done | bytes 3145760 | tf_op jit(solution)/shard_map/all_to_all | solution.py:87
  139.0 10.7 %reduce.21 = f32[16,49152]{1,0:T(8,128)} reduce(f32[16,1,49152]{2,1,0:T(1,128)S(1)} %all-to-all-done, f32[]{:T(128)} %broadcast.1324), dimensions={1}, to_apply=%all_to_all.11.reduce_sub_computation | reduce | bytes 6291460 | tf_op jit(solution)/shard_map/all_to_all | solution.py:87
  149.7 14.9 %reshape.865 = f32[2048,3,4,32]{3,2,1,0:T(4,128)} reshape(f32[16,49152]{1,0:T(8,128)} %reduce.21) | data formatting | bytes 6291456
  164.6 11.4 %copy.124 = f32[4,3,32,16,128]{4,2,1,0,3:T(8,128)} copy(f32[4,3,32,16,128]{2,0,1,4,3:T(4,128)} %bitcast.252) | data formatting | bytes 6291456 | tf_op jit(solution)/shard_map/all_to_all | solution.py:87
  183.3 14.0 %fusion.34 = (f32[256,4096]{0,1:T(8,128)}, f32[256,4096]{0,1:T(8,128)}, f32[256,4096]{0,1:T(8,128)}, f32[256,4096]{0,1:T(8,128)S(1)}) fusion(s32[256]{0:T(256)S(1)} %get-tuple-element.71, s32[256]{0:T(256)S(1)} %get-tuple-element.70, f32[4096]{0:T(1024)S(1)} %multiply_bitcast_fusion, s32[4096]{0:T(1024)S(1)} %get-tuple-element.210, ...), kind=kLoop, calls=%fused_computation.62 | loop fusion | flops 67108864 | bytes 16834560 | tf_op jit(solution)/shard_map/square | solution.py:51
  202.8 12.6 %copy.127 = f32[256,12288]{1,0:T(8,128)} copy(f32[256,12288]{0,1:T(8,128)} %bitcast.247) | data formatting | bytes 25165824 | tf_op jit(solution)/shard_map/mul | solution.py:72
  219.8 39.3 %all-gather.9.cloned.1.call-done = f32[32768,64]{0,1:T(8,128)} async-done(((f32[256,64]{0,1:T(8,128)}), f32[32768,64]{0,1:T(8,128)}) %all-gather.9.cloned.1.call-update) | async-done | bytes 8388624 | tf_op jit(solution)/shard_map/all_gather | solution.py:125
  259.2 5.9 copy.144
  274.1 11.7 %cholesky.214 = f32[128,128]{1,0:T(8,128)S(1)} custom-call(f32[128,128]{1,0:T(8,128)S(1)} %cholesky.346), custom_call_target="Cholesky" | custom-call | tf_op jit(solution)/shard_map/jit(cholesky)/cholesky | solution.py:61
  287.0 10.6 %custom-call.19 = f32[1,128,128]{1,2,0:T(8,128)S(1)} custom-call(f32[1,128,128]{2,1,0:T(8,128)} %get-tuple-element.179), custom_call_target="InvertDiagBlocksLowerTriangular" | custom-call | tf_op jit(solution)/shard_map/jit(cholesky)/cholesky | solution.py:61
  300.4 12.7 %cholesky.231 = f32[128,128]{1,0:T(8,128)S(1)} custom-call(f32[128,128]{1,0:T(8,128)} %convolution_subtract_fusion.3), custom_call_target="Cholesky" | custom-call | tf_op jit(solution)/shard_map/jit(cholesky)/cholesky | solution.py:61
  323.4 21.1 %custom-call.20 = f32[2,128,128]{1,2,0:T(8,128)} custom-call(f32[2,128,128]{2,1,0:T(8,128)} %get-tuple-element.33), custom_call_target="InvertDiagBlocksLowerTriangular" | custom-call | tf_op jit(solution)/shard_map/jit(_cho_solve)/triangular_solve | solution.py:63
  350.0 13.2 %fusion.3 = f32[256,12288]{1,0:T(8,128)S(1)} fusion(f32[256,12288]{1,0:T(8,128)} %copy.127, f32[256,64]{0,1:T(8,128)S(1)} %broadcast_subtract_fusion.3, f32[64,12288]{1,0:T(8,128)S(1)} %reshape.826, f32[12288]{0:T(1024)} %bitcast.264), kind=kOutput, calls=%fused_computation.15 | convolution fusion | flops 2422996992 | bytes 28426240 | tf_op jit(solution)/shard_map/dot_general | solution.py:71
  363.2 9.6 %fusion.258 = (f32[12288]{0:T(1024)S(1)}, f32[64,12288]{1,0:T(8,128)S(1)}) fusion(f32[64,12288]{1,0:T(8,128)} %copy-done.1, f32[256,12288]{1,0:T(8,128)S(1)} %fusion.3, f32[128,65]{0,1:T(8,128)S(1)} %fusion.160, f32[128,65]{0,1:T(8,128)S(1)} %fusion.158, f32[256]{0:T(256)S(1)} %bitcast.269), kind=kOutput, calls=%fused_computation.449 | convolution fusion | flops 2417528832 | bytes 18991104 | tf_op jit(solution)/shard_map/dot_general | solution.py:75
  376.1 7.7 mul.353
  383.8 12.6 %copy.130 = f32[256,12288]{1,0:T(8,128)} copy(f32[256,12288]{0,1:T(8,128)} %bitcast.248) | data formatting | bytes 25165824 | tf_op jit(solution)/shard_map/mul | solution.py:72
  397.6 51.6 %all-gather.11.cloned.1.call-done = f32[32768,64]{0,1:T(8,128)} async-done(((f32[256,64]{0,1:T(8,128)}), f32[32768,64]{0,1:T(8,128)}) %all-gather.11.cloned.1.call-update) | async-done | bytes 8388624 | tf_op jit(solution)/shard_map/all_gather | solution.py:125
  449.2 5.9 copy.145
  464.1 11.7 %cholesky.248 = f32[128,128]{1,0:T(8,128)S(1)} custom-call(f32[128,128]{1,0:T(8,128)S(1)} %cholesky.349), custom_call_target="Cholesky" | custom-call | tf_op jit(solution)/shard_map/jit(cholesky)/cholesky | solution.py:61
  477.0 10.6 %custom-call.21 = f32[1,128,128]{1,2,0:T(8,128)S(1)} custom-call(f32[1,128,128]{2,1,0:T(8,128)} %get-tuple-element.175), custom_call_target="InvertDiagBlocksLowerTriangular" | custom-call | tf_op jit(solution)/shard_map/jit(cholesky)/cholesky | solution.py:61
  490.4 12.7 %cholesky.265 = f32[128,128]{1,0:T(8,128)S(1)} custom-call(f32[128,128]{1,0:T(8,128)} %convolution_subtract_fusion.2), custom_call_target="Cholesky" | custom-call | tf_op jit(solution)/shard_map/jit(cholesky)/cholesky | solution.py:61
  507.9 6.2 while.9
  514.0 21.1 %custom-call.22 = f32[2,128,128]{1,2,0:T(8,128)} custom-call(f32[2,128,128]{2,1,0:T(8,128)} %get-tuple-element.34), custom_call_target="InvertDiagBlocksLowerTriangular" | custom-call | tf_op jit(solution)/shard_map/jit(_cho_solve)/triangular_solve | solution.py:63
  540.0 13.2 %fusion.2 = f32[256,12288]{1,0:T(8,128)S(1)} fusion(f32[256,12288]{1,0:T(8,128)} %copy.130, f32[256,64]{0,1:T(8,128)S(1)} %broadcast_subtract_fusion.2, f32[64,12288]{1,0:T(8,128)S(1)} %get-tuple-element.195, f32[12288]{0:T(1024)} %broadcast_multiply_fusion.10), kind=kOutput, calls=%fused_computation.13 | convolution fusion | flops 2422996992 | bytes 28426240 | tf_op jit(solution)/shard_map/dot_general | solution.py:71
  553.2 9.6 %fusion.259 = (f32[12288]{0:T(1024)S(1)}, f32[64,12288]{1,0:T(8,128)S(1)}) fusion(f32[64,12288]{1,0:T(8,128)} %copy-done, f32[256,12288]{1,0:T(8,128)S(1)} %fusion.2, f32[128,65]{0,1:T(8,128)S(1)} %fusion.164, f32[128,65]{0,1:T(8,128)S(1)} %fusion.162, f32[256]{0:T(256)S(1)} %bitcast.270), kind=kOutput, calls=%fused_computation.450 | convolution fusion | flops 2417528832 | bytes 18991104 | tf_op jit(solution)/shard_map/dot_general | solution.py:75
  566.1 7.7 mul.360
  573.8 12.6 %copy.133 = f32[256,12288]{1,0:T(8,128)} copy(f32[256,12288]{0,1:T(8,128)} %bitcast.249) | data formatting | bytes 25165824 | tf_op jit(solution)/shard_map/mul | solution.py:72
  587.6 51.6 %all-gather.13.cloned.1.call-done = f32[32768,64]{0,1:T(8,128)} async-done(((f32[256,64]{0,1:T(8,128)}), f32[32768,64]{0,1:T(8,128)}) %all-gather.13.cloned.1.call-update) | async-done | bytes 8388624 | tf_op jit(solution)/shard_map/all_gather | solution.py:125
  654.1 11.7 %cholesky.282 = f32[128,128]{1,0:T(8,128)S(1)} custom-call(f32[128,128]{1,0:T(8,128)S(1)} %cholesky.352), custom_call_target="Cholesky" | custom-call | tf_op jit(solution)/shard_map/jit(cholesky)/cholesky | solution.py:61
  666.4 10.6 %custom-call.23 = f32[1,128,128]{1,2,0:T(8,128)S(1)} custom-call(f32[1,128,128]{2,1,0:T(8,128)} %get-tuple-element.171), custom_call_target="InvertDiagBlocksLowerTriangular" | custom-call | tf_op jit(solution)/shard_map/jit(cholesky)/cholesky | solution.py:61
  679.9 12.7 %cholesky.299 = f32[128,128]{1,0:T(8,128)S(1)} custom-call(f32[128,128]{1,0:T(8,128)} %convolution_subtract_fusion.1), custom_call_target="Cholesky" | custom-call | tf_op jit(solution)/shard_map/jit(cholesky)/cholesky | solution.py:61
  696.8 6.3 while.10
  703.1 21.1 %custom-call.24 = f32[2,128,128]{1,2,0:T(8,128)} custom-call(f32[2,128,128]{2,1,0:T(8,128)} %get-tuple-element.35), custom_call_target="InvertDiagBlocksLowerTriangular" | custom-call | tf_op jit(solution)/shard_map/jit(_cho_solve)/triangular_solve | solution.py:63
  729.1 13.2 %fusion.1 = f32[256,12288]{1,0:T(8,128)S(1)} fusion(f32[256,12288]{1,0:T(8,128)} %copy.133, f32[256,64]{0,1:T(8,128)S(1)} %broadcast_subtract_fusion.1, f32[64,12288]{1,0:T(8,128)S(1)} %get-tuple-element.199, f32[12288]{0:T(1024)} %broadcast_multiply_fusion.9), kind=kOutput, calls=%fused_computation.11 | convolution fusion | flops 2422996992 | bytes 28426240 | tf_op jit(solution)/shard_map/dot_general | solution.py:71
  742.3 8.0 fusion.260
  755.1 7.7 mul.367
  762.8 12.6 %copy.136 = f32[256,12288]{1,0:T(8,128)} copy(f32[256,12288]{0,1:T(8,128)} %bitcast.250) | data formatting | bytes 25165824 | tf_op jit(solution)/shard_map/mul | solution.py:72
  776.1 52.2 %all-gather.15.cloned.1.call-done = f32[32768,64]{0,1:T(8,128)} async-done(((f32[256,64]{0,1:T(8,128)}), f32[32768,64]{0,1:T(8,128)}) %all-gather.15.cloned.1.call-update) | async-done | bytes 8388624 | tf_op jit(solution)/shard_map/all_gather | solution.py:125
  843.2 11.7 %cholesky.316 = f32[128,128]{1,0:T(8,128)S(1)} custom-call(f32[128,128]{1,0:T(8,128)S(1)} %cholesky.355), custom_call_target="Cholesky" | custom-call | tf_op jit(solution)/shard_map/jit(cholesky)/cholesky | solution.py:61
  855.6 10.6 %custom-call.25 = f32[1,128,128]{1,2,0:T(8,128)S(1)} custom-call(f32[1,128,128]{2,1,0:T(8,128)} %get-tuple-element.167), custom_call_target="InvertDiagBlocksLowerTriangular" | custom-call | tf_op jit(solution)/shard_map/jit(cholesky)/cholesky | solution.py:61
  869.0 12.7 %cholesky.333 = f32[128,128]{1,0:T(8,128)S(1)} custom-call(f32[128,128]{1,0:T(8,128)} %convolution_subtract_fusion), custom_call_target="Cholesky" | custom-call | tf_op jit(solution)/shard_map/jit(cholesky)/cholesky | solution.py:61
  886.0 6.6 while.11
  892.6 21.1 %custom-call.26 = f32[2,128,128]{1,2,0:T(8,128)} custom-call(f32[2,128,128]{2,1,0:T(8,128)} %get-tuple-element.36), custom_call_target="InvertDiagBlocksLowerTriangular" | custom-call | tf_op jit(solution)/shard_map/jit(_cho_solve)/triangular_solve | solution.py:63
  918.6 13.4 %fusion = f32[256,12288]{1,0:T(8,128)S(1)} fusion(f32[256,12288]{1,0:T(8,128)} %copy.136, f32[256,64]{0,1:T(8,128)S(1)} %broadcast_subtract_fusion, f32[64,12288]{1,0:T(8,128)S(1)} %copy-done.3, f32[12288]{0:T(1024)} %broadcast_multiply_fusion.8), kind=kOutput, calls=%fused_computation.9 | convolution fusion | flops 2422996992 | bytes 28426240 | tf_op jit(solution)/shard_map/dot_general | solution.py:71
  932.0 7.9 fusion.60
  (293 shorter events, 221.4 us)
Async XLA Ops:
  8.7 5.4 copy-start.4
  9.5 4.3 collective-permute-start
  10.8 3.3 collective-permute-start.1
  18.6 4.7 collective-permute-start.2
  22.4 1.2 collective-permute-start.3
  25.7 4.2 collective-permute-start.4
  29.1 1.2 collective-permute-start.5
  33.5 4.2 collective-permute-start.6
  36.8 1.2 collective-permute-start.7
  39.8 4.2 collective-permute-start.8
  43.2 1.2 collective-permute-start.9
  48.0 4.2 collective-permute-start.10
  51.4 1.2 collective-permute-start.11
  54.3 4.2 collective-permute-start.12
  57.7 1.2 collective-permute-start.13
  62.0 4.2 collective-permute-start.14
  65.4 1.2 collective-permute-start.15
  92.9 8.0 copy-start.20
  92.9 45.6 %all-to-all-start = ((f32[16,1,49152]{2,1,0:T(1,128)}), f32[16,1,49152]{2,1,0:T(1,128)S(1)}, u32[]{:S(2)}, u32[]{:S(2)}) async-start(f32[16,1,49152]{2,1,0:T(1,128)} %reshape.864), calls=%async_computation | async-start | bytes 6291456 | tf_op jit(solution)/shard_map/all_to_all | solution.py:87
  100.6 158.6 %all-gather.9.cloned.1.call-start = ((), (), s32[]{:S(2)}) async-start(), calls=%async_computation.1 | async-start | bytes 8454144 | tf_op jit(solution)/shard_map/all_gather | solution.py:125
  176.0 7.2 copy-start.13
  178.9 171.1 %copy-start.1 = (f32[64,12288]{1,0:T(8,128)}, f32[64,12288]{1,0:T(8,128)S(1)}, u32[]{:S(2)}) copy-start(f32[64,12288]{1,0:T(8,128)S(1)} %reshape.826) | copy-start | bytes 9437188
  182.1 267.1 %all-gather.11.cloned.1.call-start = ((), (), s32[]{:S(2)}) async-start(), calls=%async_computation.2 | async-start | bytes 8454144 | tf_op jit(solution)/shard_map/all_gather | solution.py:125
  183.3 14.0 %copy-start.14 = (s32[256]{0:T(256)}, s32[256]{0:T(256)S(1)}, u32[]{:S(2)}) copy-start(s32[256]{0:T(256)S(1)} %get-tuple-element.208) | copy-start | bytes 3076
  202.8 13.7 %copy-start.21 = (f32[4,256]{1,0:T(4,128)S(1)}, f32[4,256]{1,0:T(4,128)}, u32[]{:S(2)}) copy-start(f32[4,256]{1,0:T(4,128)} %param.14) | copy-start | bytes 12292
  313.2 2.5 copy-start.5
  323.4 39.8 %copy-start.28 = (s32[2,2]{1,0:T(2,128)}, s32[2,2]{1,0:T(2,128)S(1)}, u32[]{:S(2)}) copy-start(s32[2,2]{1,0:T(2,128)S(1)} %get-tuple-element.444) | copy-start | bytes 52
  363.2 9.6 %copy-start.22 = (s32[256]{0:T(256)S(1)}, s32[256]{0:T(256)}, u32[]{:S(2)}) copy-start(s32[256]{0:T(256)} %subtract_add_fusion.2) | copy-start | bytes 3076
  363.2 9.6 %copy-start.27 = (pred[256]{0:T(512)(128)(4,1)S(1)}, pred[256]{0:T(512)(128)(4,1)}, u32[]{:S(2)}) copy-start(pred[256]{0:T(512)(128)(4,1)} %get-tuple-element.75) | copy-start | bytes 772
  372.8 167.2 %copy-start = (f32[64,12288]{1,0:T(8,128)}, f32[64,12288]{1,0:T(8,128)S(1)}, u32[]{:S(2)}) copy-start(f32[64,12288]{1,0:T(8,128)S(1)} %get-tuple-element.195) | copy-start | bytes 9437188
  376.0 263.2 %all-gather.13.cloned.1.call-start = ((), (), s32[]{:S(2)}) async-start(), calls=%async_computation.3 | async-start | bytes 8454144 | tf_op jit(solution)/shard_map/all_gather | solution.py:125
  383.8 12.6 %copy-start.15 = (s32[256]{0:T(256)S(1)}, s32[256]{0:T(256)}, u32[]{:S(2)}) copy-start(s32[256]{0:T(256)} %copy-done.14) | copy-start | bytes 3076
  457.0 4.1 copy-start.18
  461.0 74.2 %copy-start.19 = (f32[4,256]{1,0:T(4,128)S(1)}, f32[4,256]{1,0:T(4,128)}, u32[]{:S(2)}) copy-start(f32[4,256]{1,0:T(4,128)} %param.13) | copy-start | bytes 12292
  463.4 0.7 copy-start.10
  503.2 3.0 copy-start.6
  553.2 9.6 %copy-start.24 = (s32[256]{0:T(256)S(1)}, s32[256]{0:T(256)}, u32[]{:S(2)}) copy-start(s32[256]{0:T(256)} %subtract_add_fusion.1) | copy-start | bytes 3076
  553.2 9.6 %copy-start.26 = (pred[256]{0:T(512)(128)(4,1)S(1)}, pred[256]{0:T(512)(128)(4,1)}, u32[]{:S(2)}) copy-start(pred[256]{0:T(512)(128)(4,1)} %get-tuple-element.206) | copy-start | bytes 772
  566.0 262.3 %all-gather.15.cloned.1.call-start = ((), (), s32[]{:S(2)}) async-start(), calls=%async_computation.4 | async-start | bytes 8454144 | tf_op jit(solution)/shard_map/all_gather | solution.py:125
  647.0 4.1 copy-start.17
  692.6 2.5 copy-start.7
  742.3 9.7 %copy-start.23 = (s32[256]{0:T(256)S(1)}, s32[256]{0:T(256)}, u32[]{:S(2)}) copy-start(s32[256]{0:T(256)} %subtract_add_fusion) | copy-start | bytes 3076
  742.3 9.7 %copy-start.25 = (pred[256]{0:T(512)(128)(4,1)S(1)}, pred[256]{0:T(512)(128)(4,1)}, u32[]{:S(2)}) copy-start(pred[256]{0:T(512)(128)(4,1)} %get-tuple-element.69) | copy-start | bytes 772
  750.3 1.7 copy-start.2
  836.1 4.1 copy-start.16
  840.1 78.5 %copy-start.3 = (f32[64,12288]{1,0:T(8,128)S(1)}, f32[64,12288]{1,0:T(8,128)}, u32[]{:S(2)}) copy-start(f32[64,12288]{1,0:T(8,128)} %copy-done.2) | copy-start | bytes 9437188
  842.5 0.7 copy-start.12
  881.8 2.6 copy-start.8
  (2 other events, 1.4 us)
Sparse Core Ops, SparseCore 0:
  182.2 76.9 all-gather.8
  376.1 73.0 all-gather.10
  566.1 73.0 all-gather.12
  755.2 73.0 all-gather.14
